TPU v7x, 32 devices: a whole 2x2x4 slice. The times are simulated.
32 devices in a mesh: tm: 8 (over z, y), grp: 4 (over x, core).
Axes of the slice: x: 2, y: 2, z: 4, core: 2. Of those that a mesh axis runs over, the one named last changes fastest.
Arguments:
- features: bfloat16 [4, 8192, 512], P('grp', 'tm'), may hold values from -6 to 6
- conv5_weight: bfloat16 [1536, 512], replicated, may hold values from -0.15625 to 0.15625
- conv6_weight: bfloat16 [1024, 512], replicated, may hold values from -0.1875 to 0.1875
- conv7_weight: bfloat16 [1024, 512], replicated, may hold values from -0.1875 to 0.1875
- conv5_gain: float32 [512], replicated, may hold values from 0.25 to 1.75
- conv6_gain: float32 [512], replicated, may hold values from 0.25 to 1.75
- conv7_gain: float32 [512], replicated, may hold values from 0.25 to 1.75
- proj_gain: float32 [512], replicated, may hold values from 0.25 to 1.75
- proj_weight: bfloat16 [512, 1280], replicated, may hold values from -0.25 to 0.25
- proj_bias: float32 [1280], replicated, may hold values from -3 to 3
- pos_weight: bfloat16 [16, 128, 80, 80], P('grp'), may hold values from -0.0625 to 0.0625
- pos_bias: float32 [1280], P('grp'), may hold values from -3 to 3
- out_gain: float32 [1280], P('grp'), may hold values from 0.25 to 1.75
- out_bias: float32 [1280], P('grp'), may hold values from -3 to 3
- lengths: int32 [4], P('grp'), may hold values from 512 to 1024
- crops: int32 [4], P('grp'), may hold values from 0 to 511
Outputs:
- encoded: bfloat16 [4, 1024, 1280], P(None, 'tm', 'grp')
All inputs are finite; a program needn't handle non-finite values.
Results may differ from a plain program's by a relative error of at most 0.0067.
Values may be sent and summed in bfloat16 or wider, within the bound.
No kernel may reach another device: no remote copies, remote signals or barrier semaphores. Data moves between devices by JAX's collectives and lax.ppermute only.
A program may use at most 128 MiB of HBM per device.

v0:
```python
import functools

import jax
import jax.numpy as jnp
from jax import lax
from jax.experimental import pallas as pl
from jax.experimental.pallas import tpu as pltpu
from jax.sharding import PartitionSpec as P

epsilon = 1e-05
f32 = jnp.float32
bf16 = jnp.bfloat16
TUP = 3
LANES = 256
MIB = 1 << 20


def gelu(x):
    return 0.5 * x * (1.0 + lax.erf(x * 0.7071067811865476))


def layer_norm(values, gain):
    centre = jnp.mean(values, -1, keepdims=True)
    centred = values - centre
    spread = jnp.mean(centred * centred, -1, keepdims=True)
    return centred * lax.rsqrt(spread + epsilon) * gain


def dot(a, b):
    return jnp.dot(a, b, preferred_element_type=f32)


def put(columns, first, value, stride=None):
    for c in range(columns.shape[0]):
        at = pl.ds(first, value.shape[0], stride=stride)
        columns[c, at, :] = value[:, c * 128 : (c + 1) * 128]


def take(columns, first, count, stride):
    return jnp.concatenate(
        [columns[c, pl.ds(first, count, stride=stride), :] for c in range(columns.shape[0])], 1
    )


def front_kernel(feat, nxt, w5, w6, w7, *refs):
    *gains, out, rows, block, v5, v6, v7, sems = refs
    gains = [g[...].reshape(1, -1) for g in gains]
    n = block.shape[0]
    f = n // 8
    sources = (feat.at[0], w5, w6, w7)
    copies = [
        pltpu.make_async_copy(source, target, sems.at[i])
        for i, (source, target) in enumerate(zip(sources, (block, v5, v6, v7)))
    ]
    for copy in copies:
        copy.start()
    copies[0].wait()
    put(rows, 0, block[...].astype(f32))
    put(rows, n, nxt[0].astype(f32))
    x = [take(rows, k, f, 8).astype(bf16) for k in range(9)]
    joined = jnp.concatenate(
        [jnp.concatenate(x[k : k + 7 : 2], 0) for k in range(3)], 1
    )
    copies[1].wait()
    h = gelu(layer_norm(dot(joined, v5[...]), gains[0])).astype(bf16)
    for layer, weight in ((1, v6), (2, v7)):
        count = h.shape[0] // f
        joined = jnp.concatenate(
            [
                jnp.concatenate([h[i * f : (i + 1) * f] for i in range(k, count, 2)], 0)
                for k in range(2)
            ],
            1,
        )
        copies[1 + layer].wait()
        h = gelu(layer_norm(dot(joined, weight[...]), gains[layer])).astype(bf16)
    out[...] = layer_norm(h.astype(f32), gains[3]).astype(bf16)


def front(features, nxt, weights, gains):
    rows, width = features.shape[1:]
    frames = rows // 8
    far = pl.BlockSpec(memory_space=pltpu.MemorySpace.HBM)
    flops = sum(2 * w.shape[0] * w.shape[1] * frames * m for w, m in zip(weights, (4, 2, 1)))
    return pl.pallas_call(
        front_kernel,
        grid=(1,),
        in_specs=[
            far,
            pl.BlockSpec(nxt.shape, lambda i: (0, 0, 0)),
            *[far] * 3,
            *[pl.BlockSpec(g.shape, lambda i: (0,)) for g in gains],
        ],
        out_specs=pl.BlockSpec((frames, width), lambda i: (0, 0)),
        out_shape=jax.ShapeDtypeStruct((frames, width), bf16),
        scratch_shapes=[
            pltpu.VMEM((width // 128, rows + 8, 128), f32),
            pltpu.VMEM((rows, width), bf16),
            *[pltpu.VMEM(w.shape, bf16) for w in weights],
            pltpu.SemaphoreType.DMA((4,)),
        ],
        cost_estimate=pl.CostEstimate(
            flops=4 * flops, transcendentals=0, bytes_accessed=8 * MIB
        ),
        name="front",
    )(features, nxt, *weights, *gains)


def project_kernel(n_dest, groups, tuples, half_kernel, crops, lengths, b0, b1, b2, w, bias, *rest):
    outs, rows = rest[:n_dest], rest[n_dest]
    frames = b0.shape[0]
    crop, length = crops[0], lengths[0]
    rem = lax.rem(crop - half_kernel + 2 * half_kernel * frames, frames)
    first, total = lax.axis_index("tm") * frames, lax.axis_size("tm") * frames
    me = lax.axis_index("grp")
    rows[:, 0:8, :] = jnp.zeros((rows.shape[0], 8, 128), f32)
    for i, b in enumerate((b0, b1, b2)):
        put(rows, 8 + i * frames, b[...].astype(f32))
    rows[:, 8 + 3 * frames :, :] = jnp.zeros((rows.shape[0], 16, 128), f32)
    lead = TUP - 1
    parts = []
    for a in range(TUP):
        picked = take(rows, 8 - lead + a + rem, tuples, TUP).astype(bf16)
        value = dot(picked, w[...]) + bias[...].reshape(1, -1)
        x = TUP * lax.broadcasted_iota(jnp.int32, (tuples, 1), 0) + a
        j = first - half_kernel - lead + x
        s = j + crop
        s = jnp.where(s >= total, s - total, s)
        good = (x >= lead) & (x < lead + frames + 2 * half_kernel) & (j >= 0) & (j < total)
        good = good & (s < length)
        parts.append(jnp.where(good, value, 0.0).astype(bf16))
    width = w.shape[1] // n_dest
    gw = width // groups
    pad = jnp.zeros((tuples, LANES - TUP * gw), bf16)
    for dest in range(n_dest):
        pieces = []
        for g in range(groups):
            at = dest * width + g * gw
            pieces.append(
                jnp.concatenate([p[:, at : at + gw] for p in parts] + [pad], 1)
            )
        for d in range(n_dest):

            @pl.when(me == dest ^ d)
            def _(d=d, pieces=pieces):
                for g in range(groups):
                    outs[d][g] = pieces[g]


def project(blocks, w, bias, crops, lengths, n_dest, groups, tuples, half_kernel):
    frames, width = blocks[0].shape
    whole = lambda a: pl.BlockSpec(a.shape, lambda i, *s: (0,) * a.ndim)
    shape = (groups, tuples, LANES)
    return pl.pallas_call(
        functools.partial(project_kernel, n_dest, groups, tuples, half_kernel),
        grid_spec=pltpu.PrefetchScalarGridSpec(
            num_scalar_prefetch=2,
            grid=(1,),
            in_specs=[*[whole(b) for b in blocks], whole(w), whole(bias)],
            out_specs=[pl.BlockSpec(shape, lambda i, *s: (0, 0, 0))] * n_dest,
            scratch_shapes=[pltpu.VMEM((width // 128, 3 * frames + 24, 128), f32)],
        ),
        out_shape=[jax.ShapeDtypeStruct(shape, bf16)] * n_dest,
        compiler_params=pltpu.CompilerParams(vmem_limit_bytes=40 * MIB),
        name="project_window",
    )(crops, lengths, *blocks, w, bias)


def by_tap_kernel(w, out, wide):
    gw, taps = w.shape[1], w.shape[3]
    none = jnp.zeros((128 - gw, taps), f32)

    def one(i, carry):
        put(wide, i, jnp.concatenate([w[0, i].astype(f32), none], 0).T, gw)
        return carry

    lax.fori_loop(0, gw, one, 0, unroll=20)
    step = 4 * gw
    for first in range(0, taps * gw, step):
        out[0, first : first + step, :] = wide[0, first : first + step, :].astype(bf16)


def by_tap(by_channel, first, count):
    _, gw, _, taps = by_channel.shape
    return pl.pallas_call(
        by_tap_kernel,
        grid=(count,),
        in_specs=[pl.BlockSpec((1, gw, gw, taps), lambda g: (g + first, 0, 0, 0))],
        out_specs=pl.BlockSpec((1, taps * gw, 128), lambda g: (g, 0, 0)),
        out_shape=jax.ShapeDtypeStruct((count, taps * gw, 128), bf16),
        scratch_shapes=[pltpu.VMEM((1, taps * gw, 128), f32)],
        cost_estimate=pl.CostEstimate(
            flops=0, transcendentals=0, bytes_accessed=count * taps * gw * 128 * 8
        ),
        name="by_tap_%d" % first,
    )(by_channel)


def pos_conv_kernel(n_rec, early, phases, step, tiles, gw, frames, centre, *refs):
    parts, refs = refs[:n_rec], refs[n_rec:]
    flat_a, flat_b, bias, summed, sums, flat, wide, x_f32, x_b, s_f32, plain, sems = refs
    me = lax.axis_index("grp")
    taps = flat_a.shape[1] // gw
    groups = s_f32.shape[0]
    lanes = n_rec * phases
    depth = step + tiles
    m = step * lanes
    n = TUP * gw
    g = pl.program_id(0)
    slot = lax.rem(g, 2)

    def fetch(i):
        source = flat_a.at[i] if i < early else flat_b.at[i - early]
        pltpu.make_async_copy(source, flat.at[i % 2], sems.at[i % 2]).start()

    @pl.when(g == 0)
    def _():
        for i in range(min(2, groups)):
            fetch(i)

    for d in range(n_rec):
        wide[0 : parts[d].shape[1], :] = parts[d][0].astype(f32)
        rec = me ^ d
        for p in range(phases):
            put(x_f32, rec * phases + p, wide[p * step : p * step + depth, :], lanes)
    for c in range(LANES // 128):
        x_b[:, c * 128 : (c + 1) * 128] = x_f32[c, 0 : depth * lanes, :].astype(bf16)
    zero = jnp.zeros((gw, gw), bf16)

    pltpu.make_async_copy(flat_a.at[0], flat.at[slot], sems.at[slot]).wait()
    total = jnp.zeros((m, LANES), f32)
    for j in range(tiles):
        cols = []
        for b in range(TUP):
            taps_of = [TUP * j + a - b - (TUP - 1) for a in range(TUP)]
            cols.append(
                jnp.concatenate(
                    [
                        flat[slot, k * gw : (k + 1) * gw, 0:gw] if 0 <= k < taps else zero
                        for k in taps_of
                    ],
                    0,
                )
            )
        cols.append(jnp.zeros((n, LANES - n), bf16))
        total = total + dot(x_b[lanes * j : lanes * j + m, 0:n], jnp.concatenate(cols, 1))
    for i in range(2, groups):

        @pl.when(g == i - 2)
        def _(i=i):
            fetch(i)

    own = x_b[lanes * centre : lanes * centre + m, :].astype(f32)
    rows = [bias[...].reshape(1, -1)[:, i * gw : (i + 1) * gw] for i in range(groups)]
    gap = jnp.zeros((1, LANES - n), f32)
    shift = jnp.zeros((1, LANES), f32)
    for i in range(groups):
        shift = jnp.where(g == i, jnp.concatenate([rows[i]] * TUP + [gap], 1), shift)
    put(s_f32.at[g], 0, own + gelu(total + shift))

    @pl.when(g == groups - 1)
    def _():
        share = TUP * step
        for r in range(n_rec):
            for p in range(phases):
                rows = [take(s_f32.at[i], r * phases + p, step, lanes) for i in range(groups)]
                for b in range(TUP):
                    count = -(-(min(share, frames - p * share) - b) // TUP)
                    line = jnp.concatenate([v[:, b * gw : (b + 1) * gw] for v in rows], 1)
                    gap = plain.shape[0] * 128 - groups * gw
                    line = jnp.concatenate([line, jnp.zeros((step, gap), f32)], 1)
                    put(plain, r * frames + p * share + b, line[0:count], TUP)
        for r in range(n_rec):
            first = jnp.zeros((1, frames), f32)
            second = jnp.zeros((1, frames), f32)
            for c in range(plain.shape[0]):
                end = min(groups * gw, (c + 1) * 128)
                turned = plain[c, r * frames : (r + 1) * frames, :].T[0 : end - c * 128]
                summed[r, c * 128 : end, :] = turned
                first = first + jnp.sum(turned, 0, keepdims=True)
                second = second + jnp.sum(turned * turned, 0, keepdims=True)
            sums[r : r + 1, :] = first
            sums[n_rec + r : n_rec + r + 1, :] = second


def pos_conv(parts, flat_a, flat_b, bias, n_rec, frames, tiles, gw, centre):
    early = flat_a.shape[0]
    groups = early + flat_b.shape[0]
    phases = 16 // n_rec
    step = -(-(frames // phases) // TUP)
    depth = step + tiles
    tuples = parts[0].shape[1]
    lanes = 16
    width = groups * gw
    return pl.pallas_call(
        functools.partial(pos_conv_kernel, n_rec, early, phases, step, tiles, gw, frames, centre),
        grid=(groups,),
        in_specs=[
            *[pl.BlockSpec((1, tuples, LANES), lambda g: (g, 0, 0))] * n_rec,
            *[pl.BlockSpec(memory_space=pltpu.MemorySpace.HBM)] * 2,
            pl.BlockSpec(bias.shape, lambda g: (0,)),
        ],
        out_specs=[
            pl.BlockSpec((n_rec, width, frames), lambda g: (0, 0, 0)),
            pl.BlockSpec((2 * n_rec, frames), lambda g: (0, 0)),
        ],
        scratch_shapes=[
            pltpu.VMEM((2, *flat_a.shape[1:]), bf16),
            pltpu.VMEM((tuples + 16, LANES), f32),
            pltpu.VMEM((LANES // 128, (depth + 9) * lanes, 128), f32),
            pltpu.VMEM((depth * lanes, LANES), bf16),
            pltpu.VMEM((groups, LANES // 128, (step + 9) * lanes, 128), f32),
            pltpu.VMEM((-(-width // 128), n_rec * frames + 64, 128), f32),
            pltpu.SemaphoreType.DMA((2,)),
        ],
        out_shape=[
            jax.ShapeDtypeStruct((n_rec, width, frames), f32),
            jax.ShapeDtypeStruct((2 * n_rec, frames), f32),
        ],
        compiler_params=pltpu.CompilerParams(vmem_limit_bytes=48 * MIB),
        name="pos_conv",
    )(*parts, flat_a, flat_b, bias)


def on_device(
    features,
    conv5_weight,
    conv6_weight,
    conv7_weight,
    conv5_gain,
    conv6_gain,
    conv7_gain,
    proj_gain,
    proj_weight,
    proj_bias,
    pos_weight,
    pos_bias,
    out_gain,
    out_bias,
    lengths,
    crops,
):
    tm, grp = lax.axis_size("tm"), lax.axis_size("grp")
    groups, taps, gw, _ = pos_weight.shape
    half_kernel = taps // 2
    frames = features.shape[1] // 8
    crop = crops[0]

    back = [(i + 1, i) for i in range(tm - 1)]
    edge = lax.ppermute(features[:, :1, :], "tm", back)
    weights = (conv5_weight, conv6_weight, conv7_weight)
    gains = (conv5_gain, conv6_gain, conv7_gain, proj_gain)
    by_channel = pos_weight.transpose(0, 2, 3, 1)
    early = groups // 2
    normed = front(features, edge, weights, gains)

    start = crop - half_kernel
    whole_blocks = jnp.floor_divide(start, frames)

    def from_block(distance):
        distance %= tm
        if distance == 0:
            return lambda v: v
        route = [((i + distance) % tm, i) for i in range(tm)]
        return lambda v: lax.ppermute(v, "tm", route)

    tiles = -(-(taps + 2 * (TUP - 1)) // TUP)

    def branch(first):
        return lambda v, w: (
            *[from_block(first + i)(v) for i in range(3)],
            by_tap(w, 0, early),
        )

    tiles = -(-(taps + 2 * (TUP - 1)) // TUP)
    lowest = -(-half_kernel // frames)
    most = tm // 2
    *blocks, flat_a = lax.switch(
        whole_blocks + lowest,
        [branch(b) for b in range(-lowest, most)],
        normed,
        by_channel,
    )

    n_rec = grp
    phases = 16 // n_rec
    step = -(-(frames // phases) // TUP)
    tuples = -(-(step * phases + tiles) // 8) * 8
    parts = project(
        blocks, proj_weight, proj_bias, crops, lengths, n_rec, groups, tuples, half_kernel
    )
    parts = [
        p if d == 0 else lax.ppermute(p, "grp", [(i ^ d, i) for i in range(grp)])
        for d, p in enumerate(parts)
    ]
    flat_b = by_tap(by_channel, early, groups - early)
    centre = (half_kernel + TUP - 1) // TUP
    summed, own = pos_conv(parts, flat_a, flat_b, pos_bias, n_rec, frames, tiles, gw, centre)
    totals = own
    for d in range(1, grp):
        totals = totals + lax.ppermute(own, "grp", [(i ^ d, i) for i in range(grp)])
    channels = proj_weight.shape[1]
    mean = totals[:n_rec] / channels
    spread = totals[n_rec:] / channels - mean * mean
    scaled = (summed - mean[:, None]) * lax.rsqrt(spread + epsilon)[:, None]
    scaled = scaled * out_gain[:, None] + out_bias[:, None]
    return scaled.astype(bf16).transpose(0, 2, 1)


def solution(mesh):
    return jax.shard_map(
        on_device,
        mesh=mesh,
        in_specs=(
            P("grp", "tm", None),
            P(),
            P(),
            P(),
            P(),
            P(),
            P(),
            P(),
            P(),
            P(),
            P("grp", None, None, None),
            P("grp"),
            P("grp"),
            P("grp"),
            P("grp"),
            P("grp"),
        ),
        out_specs=P(None, "tm", "grp"),
        check_vma=False,
    )
```

profile of v0, /device:TPU:0, one launch (start us, length us, event | category | flops | bytes accessed | tf_op | source)
XLA Modules:
  0.0 61.2 jit_solution(6053019790762721597)
XLA Ops:
  0.0 0.7 %slice.9 = bf16[1,1,512]{2,1,0:T(2,128)(2,1)S(1)} slice(bf16[1,1024,512]{2,1,0:T(8,128)(2,1)} %feat.1), slice={[0:1], [0:1], [0:512]} | slice | bytes 2048 | tf_op jit(solution)/shard_map/slice | solution.py:350
  0.7 1.3 %collective-permute-start.13 = (bf16[1,1,512]{2,1,0:T(2,128)(2,1)S(1)}, bf16[1,1,512]{2,1,0:T(2,128)(2,1)S(1)}, u32[]{:S(2)}, u32[]{:S(2)}) collective-permute-start(bf16[1,1,512]{2,1,0:T(2,128)(2,1)S(1)} %slice.9), channel_id=1, source_target_pairs={{4,0},{8,4},{12,8},{16,12},{20,16},{24,20},{28,24},{5,1},{9,5},{13... | collective-permute-start | bytes 3080 | tf_op jit(solution)/shard_map/ppermute | solution.py:350
  3.3 3.8 %collective-permute-done.13.nxt = bf16[1,1,512]{2,1,0:T(2,128)(2,1)S(1)} collective-permute-done((bf16[1,1,512]{2,1,0:T(2,128)(2,1)S(1)}, bf16[1,1,512]{2,1,0:T(2,128)(2,1)S(1)}, u32[]{:S(2)}, u32[]{:S(2)}) %collective-permute-start.13) | collective-permute-done | bytes 1056 | tf_op jit(solution)/shard_map/ppermute | solution.py:350
  7.1 0.0 copy-start.5
  7.1 0.6 copy-done.5
  7.7 5.4 %front.1 = bf16[128,512]{1,0:T(8,128)(2,1)S(1)} custom-call(bf16[1,1024,512]{2,1,0:T(8,128)(2,1)} %feat.1, bf16[1,1,512]{2,1,0:T(2,128)(2,1)} %copy-done.5, bf16[1536,512]{1,0:T(8,128)(2,1)} %w5.1, bf16[1024,512]{1,0:T(8,128)(2,1)} %w6.1, bf16[1024,512]{1,0:T(8,128)(2,1)} %w7.1, f32[512]{0:T(512)} %refs_0_.1, f32[512]{0:T(512)} %refs_1_.1, f32[512]{0:T(512)} %refs_2_.1, ...), custom_call_target="tpu_custom_call" | custom-call | flops 4831838208 | bytes 8388608 | tf_op jit(solution)/shard_map/front/pallas_call | solution.py:85
  13.1 0.0 copy-start
  13.2 0.0 copy-start.1
  13.2 11.6 %conditional.1 = (bf16[128,512]{1,0:T(8,128)(2,1)}, bf16[128,512]{1,0:T(8,128)(2,1)S(1)}, bf16[128,512]{1,0:T(8,128)(2,1)}, bf16[2,10240,128]{2,1,0:T(8,128)(2,1)}) conditional(s32[]{:T(128)} %clamp.3, (bf16[128,512]{1,0:T(8,128)(2,1)S(1)}, bf16[4,80,80,128]{3,2,1,0:T(8,128)(2,1)}) %tuple.32, ...), branch_computations={%region_0.1_spmd, %region_1.2_spmd, %region_2.3_spmd, %region_3.4_... | conditional | bytes 22806680 | solution.py:378
  13.2 3.0 %collective-permute-start = (bf16[128,512]{1,0:T(8,128)(2,1)S(1)}, bf16[128,512]{1,0:T(8,128)(2,1)}, u32[]{:S(2)}, u32[]{:S(2)}) collective-permute-start(bf16[128,512]{1,0:T(8,128)(2,1)S(1)} %get-tuple-element.58), channel_id=1, source_target_pairs={{28,0},{0,4},{4,8},{8,12},{12,16},{16,20},{20,24},{24,28},{29,1},{... | collective-permute-start | bytes 393224 | tf_op jit(solution)/shard_map/cond/branch_0_fun/ppermute | solution.py:365
  16.2 1.8 %collective-permute-start.1 = (bf16[128,512]{1,0:T(8,128)(2,1)S(1)}, bf16[128,512]{1,0:T(8,128)(2,1)}, u32[]{:S(2)}, u32[]{:S(2)}) collective-permute-start(bf16[128,512]{1,0:T(8,128)(2,1)S(1)} %get-tuple-element.58), channel_id=1, source_target_pairs={{4,0},{8,4},{12,8},{16,12},{20,16},{24,20},{28,24},{0,28},{5,1},{9... | collective-permute-start | bytes 393224 | tf_op jit(solution)/shard_map/cond/branch_0_fun/ppermute | solution.py:365
  18.0 6.8 %by_tap_0.5 = bf16[2,10240,128]{2,1,0:T(8,128)(2,1)} custom-call(bf16[4,80,80,128]{3,2,1,0:T(8,128)(2,1)} %get-tuple-element.26.w), custom_call_target="tpu_custom_call" | custom-call | bytes 20971520 | tf_op jit(solution)/shard_map/cond/branch_0_fun/by_tap_0/pallas_call | solution.py:185
  24.8 0.0 collective-permute-done
  24.8 0.0 collective-permute-done.1
  24.8 0.0 copy-done
  24.8 0.0 copy-done.1
  24.8 2.5 %project_window.1 = (bf16[4,88,256]{2,1,0:T(8,128)(2,1)S(1)}, bf16[4,88,256]{2,1,0:T(8,128)(2,1)S(1)}, bf16[4,88,256]{2,1,0:T(8,128)(2,1)S(1)}, bf16[4,88,256]{2,1,0:T(8,128)(2,1)S(1)}) custom-call(s32[1]{0:T(128)S(6)} %copy.38.crops, s32[1]{0:T(128)S(6)} %copy.37.lengths, bf16[128,512]{1,0:T(8,128)(2,1)} %get-tuple-element.45.b0, ...), custom_call_target="tpu_custom_call" | custom-call | tf_op jit(solution)/shard_map/project_window/pallas_call | solution.py:154
  27.4 1.6 %collective-permute-start.14 = (bf16[4,88,256]{2,1,0:T(8,128)(2,1)S(1)}, bf16[4,88,256]{2,1,0:T(8,128)(2,1)S(1)}, u32[]{:S(2)}, u32[]{:S(2)}) collective-permute-start(bf16[4,88,256]{2,1,0:T(8,128)(2,1)S(1)} %get-tuple-element.49), channel_id=1, source_target_pairs={{1,0},{0,1},{3,2},{2,3},{5,4},{4,5},{7,6},{6,7},{9,8},{8,9},{11,10... | collective-permute-start | bytes 540680 | tf_op jit(solution)/shard_map/ppermute | solution.py:393
  29.0 6.3 %collective-permute-start.15 = (bf16[4,88,256]{2,1,0:T(8,128)(2,1)S(1)}, bf16[4,88,256]{2,1,0:T(8,128)(2,1)S(1)}, u32[]{:S(2)}, u32[]{:S(2)}) collective-permute-start(bf16[4,88,256]{2,1,0:T(8,128)(2,1)S(1)} %get-tuple-element.50), channel_id=1, source_target_pairs={{2,0},{3,1},{0,2},{1,3},{6,4},{7,5},{4,6},{5,7},{10,8},{11,9},{8,1... | collective-permute-start | bytes 540680 | tf_op jit(solution)/shard_map/ppermute | solution.py:393
  35.3 0.0 copy-start.2
  35.3 0.1 collective-permute-start.16
  35.4 6.9 %by_tap_2.1.refs_5_ = bf16[2,10240,128]{2,1,0:T(8,128)(2,1)} custom-call(bf16[4,80,80,128]{3,2,1,0:T(8,128)(2,1)} %bitcast.9), custom_call_target="tpu_custom_call" | custom-call | bytes 20971520 | tf_op jit(solution)/shard_map/by_tap_2/pallas_call | solution.py:185
  42.2 0.0 collective-permute-done.14.refs_1_
  42.2 0.0 collective-permute-done.15.refs_2_
  42.2 1.8 %collective-permute-done.16.refs_3_ = bf16[4,88,256]{2,1,0:T(8,128)(2,1)S(1)} collective-permute-done((bf16[4,88,256]{2,1,0:T(8,128)(2,1)S(1)}, bf16[4,88,256]{2,1,0:T(8,128)(2,1)S(1)}, u32[]{:S(2)}, u32[]{:S(2)}) %collective-permute-start.16) | collective-permute-done | bytes 180256 | tf_op jit(solution)/shard_map/ppermute | solution.py:393
  44.0 0.0 copy-done.2
  44.0 0.0 copy-start.3
  44.0 0.0 copy-start.4
  44.0 11.2 %pos_conv.1 = (f32[4,320,128]{2,1,0:T(8,128)S(1)}, f32[8,128]{1,0:T(8,128)S(1)}) custom-call(bf16[4,88,256]{2,1,0:T(8,128)(2,1)S(1)} %get-tuple-element.48.refs_0_, bf16[4,88,256]{2,1,0:T(8,128)(2,1)S(1)} %collective-permute-done.14.refs_1_, bf16[4,88,256]{2,1,0:T(8,128)(2,1)S(1)} %collective-permute-done.15.refs_2_, ...), custom_call_target="tpu_custom_call" | custom-call | tf_op jit(solution)/shard_map/pos_conv/pallas_call | solution.py:295
  55.3 0.2 collective-permute-start.17
  55.5 1.7 %collective-permute-start.18 = (f32[8,128]{1,0:T(8,128)S(1)}, f32[8,128]{1,0:T(8,128)S(1)}, u32[]{:S(2)}, u32[]{:S(2)}) collective-permute-start(f32[8,128]{1,0:T(8,128)S(1)} %get-tuple-element.54), channel_id=1, source_target_pairs={{2,0},{3,1},{0,2},{1,3},{6,4},{7,5},{4,6},{5,7},{10,8},{11,9},{8,1... | collective-permute-start | bytes 12296 | tf_op jit(solution)/shard_map/ppermute | solution.py:401
  57.2 0.0 collective-permute-start.19
  57.3 0.0 collective-permute-done.17
  57.3 1.8 %collective-permute-done.18 = f32[8,128]{1,0:T(8,128)S(1)} collective-permute-done((f32[8,128]{1,0:T(8,128)S(1)}, f32[8,128]{1,0:T(8,128)S(1)}, u32[]{:S(2)}, u32[]{:S(2)}) %collective-permute-start.18) | collective-permute-done | bytes 4128 | tf_op jit(solution)/shard_map/ppermute | solution.py:401
  59.1 1.2 %collective-permute-done.19 = f32[8,128]{1,0:T(8,128)S(1)} collective-permute-done((f32[8,128]{1,0:T(8,128)S(1)}, f32[8,128]{1,0:T(8,128)S(1)}, u32[]{:S(2)}, u32[]{:S(2)}) %collective-permute-start.19) | collective-permute-done | bytes 4128 | tf_op jit(solution)/shard_map/ppermute | solution.py:401
  60.3 0.0 copy-done.3
  60.3 0.0 copy-done.4
  60.3 0.9 %fusion = bf16[4,128,320]{1,2,0:T(8,128)(2,1)} fusion(f32[4,320,128]{2,1,0:T(8,128)S(1)} %get-tuple-element.53, f32[320]{0:T(512)S(1)} %copy-done.3, f32[320]{0:T(512)S(1)} %copy-done.4, f32[4,128]{1,0:T(4,128)S(1)} %get-tuple-element.56, f32[4,128]{1,0:T(4,128)S(1)} %get-tuple-element.55), kind=kLoop, calls=%fused_computation.1 | loop fusion | flops 819200 | bytes 989696 | tf_op jit(solution)/shard_map/transpose | solution.py:407
  (2 shorter events, 0.0 us)
Async XLA Ops:
  0.7 6.4 %collective-permute-start.13 = (bf16[1,1,512]{2,1,0:T(2,128)(2,1)S(1)}, bf16[1,1,512]{2,1,0:T(2,128)(2,1)S(1)}, u32[]{:S(2)}, u32[]{:S(2)}) collective-permute-start(bf16[1,1,512]{2,1,0:T(2,128)(2,1)S(1)} %slice.9), channel_id=1, source_target_pairs={{4,0},{8,4},{12,8},{16,12},{20,16},{24,20},{28,24},{5,1},{9,5},{13... | collective-permute-start | bytes 3080 | tf_op jit(solution)/shard_map/ppermute | solution.py:350
  7.1 0.6 copy-start.5
  13.1 11.7 %copy-start = (bf16[512,1280]{1,0:T(8,128)(2,1)S(1)}, bf16[512,1280]{1,0:T(8,128)(2,1)}, u32[]{:S(2)}) copy-start(bf16[512,1280]{1,0:T(8,128)(2,1)} %w.1) | copy-start | bytes 3932164
  13.2 11.7 %copy-start.1 = (f32[1280]{0:T(1024)S(1)}, f32[1280]{0:T(1024)}, u32[]{:S(2)}) copy-start(f32[1280]{0:T(1024)} %bias.1) | copy-start | bytes 15364
  13.2 11.6 %collective-permute-start = (bf16[128,512]{1,0:T(8,128)(2,1)S(1)}, bf16[128,512]{1,0:T(8,128)(2,1)}, u32[]{:S(2)}, u32[]{:S(2)}) collective-permute-start(bf16[128,512]{1,0:T(8,128)(2,1)S(1)} %get-tuple-element.58), channel_id=1, source_target_pairs={{28,0},{0,4},{4,8},{8,12},{12,16},{16,20},{20,24},{24,28},{29,1},{... | collective-permute-start | bytes 393224 | tf_op jit(solution)/shard_map/cond/branch_0_fun/ppermute | solution.py:365
  16.2 8.6 %collective-permute-start.1 = (bf16[128,512]{1,0:T(8,128)(2,1)S(1)}, bf16[128,512]{1,0:T(8,128)(2,1)}, u32[]{:S(2)}, u32[]{:S(2)}) collective-permute-start(bf16[128,512]{1,0:T(8,128)(2,1)S(1)} %get-tuple-element.58), channel_id=1, source_target_pairs={{4,0},{8,4},{12,8},{16,12},{20,16},{24,20},{28,24},{0,28},{5,1},{9... | collective-permute-start | bytes 393224 | tf_op jit(solution)/shard_map/cond/branch_0_fun/ppermute | solution.py:365
  27.4 14.9 %collective-permute-start.14 = (bf16[4,88,256]{2,1,0:T(8,128)(2,1)S(1)}, bf16[4,88,256]{2,1,0:T(8,128)(2,1)S(1)}, u32[]{:S(2)}, u32[]{:S(2)}) collective-permute-start(bf16[4,88,256]{2,1,0:T(8,128)(2,1)S(1)} %get-tuple-element.49), channel_id=1, source_target_pairs={{1,0},{0,1},{3,2},{2,3},{5,4},{4,5},{7,6},{6,7},{9,8},{8,9},{11,10... | collective-permute-start | bytes 540680 | tf_op jit(solution)/shard_map/ppermute | solution.py:393
  29.0 13.2 %collective-permute-start.15 = (bf16[4,88,256]{2,1,0:T(8,128)(2,1)S(1)}, bf16[4,88,256]{2,1,0:T(8,128)(2,1)S(1)}, u32[]{:S(2)}, u32[]{:S(2)}) collective-permute-start(bf16[4,88,256]{2,1,0:T(8,128)(2,1)S(1)} %get-tuple-element.50), channel_id=1, source_target_pairs={{2,0},{3,1},{0,2},{1,3},{6,4},{7,5},{4,6},{5,7},{10,8},{11,9},{8,1... | collective-permute-start | bytes 540680 | tf_op jit(solution)/shard_map/ppermute | solution.py:393
  35.3 8.7 %copy-start.2 = (f32[320]{0:T(512)S(1)}, f32[320]{0:T(512)}, u32[]{:S(2)}) copy-start(f32[320]{0:T(512)} %refs_6_.1) | copy-start | bytes 3844
  35.3 8.7 %collective-permute-start.16 = (bf16[4,88,256]{2,1,0:T(8,128)(2,1)S(1)}, bf16[4,88,256]{2,1,0:T(8,128)(2,1)S(1)}, u32[]{:S(2)}, u32[]{:S(2)}) collective-permute-start(bf16[4,88,256]{2,1,0:T(8,128)(2,1)S(1)} %get-tuple-element.51), channel_id=1, source_target_pairs={{3,0},{2,1},{1,2},{0,3},{7,4},{6,5},{5,6},{4,7},{11,8},{10,9},{9,1... | collective-permute-start | bytes 540680 | tf_op jit(solution)/shard_map/ppermute | solution.py:393
  44.0 16.2 %copy-start.3 = (f32[320]{0:T(512)S(1)}, f32[320]{0:T(512)}, u32[]{:S(2)}) copy-start(f32[320]{0:T(512)} %param.34) | copy-start | bytes 3844
  44.0 16.2 %copy-start.4 = (f32[320]{0:T(512)S(1)}, f32[320]{0:T(512)}, u32[]{:S(2)}) copy-start(f32[320]{0:T(512)} %param.33) | copy-start | bytes 3844
  55.3 2.0 %collective-permute-start.17 = (f32[8,128]{1,0:T(8,128)S(1)}, f32[8,128]{1,0:T(8,128)S(1)}, u32[]{:S(2)}, u32[]{:S(2)}) collective-permute-start(f32[8,128]{1,0:T(8,128)S(1)} %get-tuple-element.54), channel_id=1, source_target_pairs={{1,0},{0,1},{3,2},{2,3},{5,4},{4,5},{7,6},{6,7},{9,8},{8,9},{11,10... | collective-permute-start | bytes 12296 | tf_op jit(solution)/shard_map/ppermute | solution.py:401
  55.5 3.6 %collective-permute-start.18 = (f32[8,128]{1,0:T(8,128)S(1)}, f32[8,128]{1,0:T(8,128)S(1)}, u32[]{:S(2)}, u32[]{:S(2)}) collective-permute-start(f32[8,128]{1,0:T(8,128)S(1)} %get-tuple-element.54), channel_id=1, source_target_pairs={{2,0},{3,1},{0,2},{1,3},{6,4},{7,5},{4,6},{5,7},{10,8},{11,9},{8,1... | collective-permute-start | bytes 12296 | tf_op jit(solution)/shard_map/ppermute | solution.py:401
  57.2 3.0 %collective-permute-start.19 = (f32[8,128]{1,0:T(8,128)S(1)}, f32[8,128]{1,0:T(8,128)S(1)}, u32[]{:S(2)}, u32[]{:S(2)}) collective-permute-start(f32[8,128]{1,0:T(8,128)S(1)} %get-tuple-element.54), channel_id=1, source_target_pairs={{3,0},{2,1},{1,2},{0,3},{7,4},{6,5},{5,6},{4,7},{11,8},{10,9},{9,1... | collective-permute-start | bytes 12296 | tf_op jit(solution)/shard_map/ppermute | solution.py:401
where the time goes:
time: 61.7 us; the launch traced here: 61.2 us
  Pallas kernels  32.9 us (53%)
  starting transfers between devices  16 us (26%)
  waiting for transfers between devices  8.61 us (14%)
  between operations  1.41 us (2%)
  local copies, waits for them, and re-layouts  1.3 us (2%)
  other arithmetic  0.93 us (2%)
    pallas_call x2, Pallas kernels, by_tap(): pl.pallas_call(by_tap_kernel, grid=(count,), in_specs=[pl.BlockSpec((1, g...  13.7 us
    pallas_call x1, Pallas kernels, pos_conv(): pl.pallas_call(functools.partial(pos_conv_kernel, n_rec, early, phases, s...  11.2 us
    ppermute x3, starting transfers between devices, on_device(): lax.ppermute(p, 'grp', [(i ^ d, i) for i in range(grp)])  7.99 us
    pallas_call x1, Pallas kernels, front(): pl.pallas_call(front_kernel, grid=(1,), in_specs=[far, pl.BlockSpec(nxt.s...  5.44 us
    ppermute x2, starting transfers between devices, from_block(): return lambda v: lax.ppermute(v, 'tm', route)  4.78 us
    ppermute x1, waiting for transfers between devices, on_device(): edge = lax.ppermute(features[:, :1, :], 'tm', back)  3.81 us
    ppermute x3, waiting for transfers between devices, on_device(): totals = totals + lax.ppermute(own, 'grp', [(i ^ d, i) for i in range(grp)])  2.98 us
    pallas_call x1, Pallas kernels, project(): pl.pallas_call(functools.partial(project_kernel, n_dest, groups, tuples,...  2.54 us
  transfers between devices with their start and end apart: 9, of which 4 were waited for; matrix products, arithmetic and copies ran while one was open for 0% of the time, Pallas kernels for 22%

commit v1 on v0

--- a/solution.py
+++ b/solution.py
@@ -43,7 +43,7 @@
 
 
 def front_kernel(feat, nxt, w5, w6, w7, *refs):
-    *gains, out, rows, block, v5, v6, v7, sems = refs
+    *gains, out, low, high, rows, block, v5, v6, v7, sems = refs
     gains = [g[...].reshape(1, -1) for g in gains]
     n = block.shape[0]
     f = n // 8
@@ -74,12 +74,16 @@
         )
         copies[1 + layer].wait()
         h = gelu(layer_norm(dot(joined, weight[...]), gains[layer])).astype(bf16)
-    out[...] = layer_norm(h.astype(f32), gains[3]).astype(bf16)
+    normed = layer_norm(h.astype(f32), gains[3]).astype(bf16)
+    out[...] = normed
+    low[...] = normed[: f // 2]
+    high[...] = normed[f // 2 :]
 
 
 def front(features, nxt, weights, gains):
     rows, width = features.shape[1:]
     frames = rows // 8
+    sizes = (frames, frames // 2, frames // 2)
     far = pl.BlockSpec(memory_space=pltpu.MemorySpace.HBM)
     flops = sum(2 * w.shape[0] * w.shape[1] * frames * m for w, m in zip(weights, (4, 2, 1)))
     return pl.pallas_call(
@@ -91,8 +95,8 @@
             *[far] * 3,
             *[pl.BlockSpec(g.shape, lambda i: (0,)) for g in gains],
         ],
-        out_specs=pl.BlockSpec((frames, width), lambda i: (0, 0)),
-        out_shape=jax.ShapeDtypeStruct((frames, width), bf16),
+        out_specs=[pl.BlockSpec((n, width), lambda i: (0, 0)) for n in sizes],
+        out_shape=[jax.ShapeDtypeStruct((n, width), bf16) for n in sizes],
         scratch_shapes=[
             pltpu.VMEM((width // 128, rows + 8, 128), f32),
             pltpu.VMEM((rows, width), bf16),
@@ -110,13 +114,18 @@
     outs, rows = rest[:n_dest], rest[n_dest]
     frames = b0.shape[0]
     crop, length = crops[0], lengths[0]
+    piece = b2.shape[0]
     rem = lax.rem(crop - half_kernel + 2 * half_kernel * frames, frames)
+    odd = rem >= piece
+    rem = jnp.where(odd, rem - piece, rem)
     first, total = lax.axis_index("tm") * frames, lax.axis_size("tm") * frames
     me = lax.axis_index("grp")
     rows[:, 0:8, :] = jnp.zeros((rows.shape[0], 8, 128), f32)
-    for i, b in enumerate((b0, b1, b2)):
-        put(rows, 8 + i * frames, b[...].astype(f32))
-    rows[:, 8 + 3 * frames :, :] = jnp.zeros((rows.shape[0], 16, 128), f32)
+    at = pl.multiple_of(jnp.where(odd, 8 + piece, 8), 8)
+    put(rows, at, b0[...].astype(f32))
+    put(rows, pl.multiple_of(at + frames, 8), b1[...].astype(f32))
+    put(rows, pl.multiple_of(jnp.where(odd, 8, 8 + 2 * frames), 8), b2[...].astype(f32))
+    rows[:, 8 + 2 * frames + piece :, :] = jnp.zeros((rows.shape[0], 16, 128), f32)
     lead = TUP - 1
     parts = []
     for a in range(TUP):
@@ -158,7 +167,7 @@
             grid=(1,),
             in_specs=[*[whole(b) for b in blocks], whole(w), whole(bias)],
             out_specs=[pl.BlockSpec(shape, lambda i, *s: (0, 0, 0))] * n_dest,
-            scratch_shapes=[pltpu.VMEM((width // 128, 3 * frames + 24, 128), f32)],
+            scratch_shapes=[pltpu.VMEM((width // 128, 2 * frames + blocks[2].shape[0] + 24, 128), f32)],
         ),
         out_shape=[jax.ShapeDtypeStruct(shape, bf16)] * n_dest,
         compiler_params=pltpu.CompilerParams(vmem_limit_bytes=40 * MIB),
@@ -352,10 +361,11 @@
     gains = (conv5_gain, conv6_gain, conv7_gain, proj_gain)
     by_channel = pos_weight.transpose(0, 2, 3, 1)
     early = groups // 2
-    normed = front(features, edge, weights, gains)
+    normed, low, high = front(features, edge, weights, gains)
 
     start = crop - half_kernel
-    whole_blocks = jnp.floor_divide(start, frames)
+    piece = frames // 2
+    pieces = jnp.floor_divide(start, piece)
 
     def from_block(distance):
         distance %= tm
@@ -364,21 +374,25 @@
         route = [((i + distance) % tm, i) for i in range(tm)]
         return lambda v: lax.ppermute(v, "tm", route)
 
+    def branch(first):
+        block, odd = first // 2, first % 2
+
+        def run(v, low, high, w):
+            pair = [from_block(block + odd + i)(v) for i in range(2)]
+            extra = from_block(block)(high) if odd else from_block(block + 2)(low)
+            return *pair, extra, by_tap(w, 0, early)
+
+        return run
+
     tiles = -(-(taps + 2 * (TUP - 1)) // TUP)
-
-    def branch(first):
-        return lambda v, w: (
-            *[from_block(first + i)(v) for i in range(3)],
-            by_tap(w, 0, early),
-        )
-
-    tiles = -(-(taps + 2 * (TUP - 1)) // TUP)
-    lowest = -(-half_kernel // frames)
-    most = tm // 2
+    lowest = -(-half_kernel // piece)
+    most = (frames * tm // 2 - 1 - half_kernel) // piece + 1
     *blocks, flat_a = lax.switch(
-        whole_blocks + lowest,
+        pieces + lowest,
         [branch(b) for b in range(-lowest, most)],
         normed,
+        low,
+        high,
         by_channel,
     )
 

time: 61.7 us -> 58.8 us (0.953)
  starting transfers between devices: 16 us -> 12.4 us
    ppermute x3, starting transfers between devices: 7.99 us -> 5.83 us  [on_device(): lax.ppermute(p, 'grp', [(i ^ d, i) for i in range(grp)])]
    ppermute x2, starting transfers between devices: 4.78 us -> 3.38 us  [from_block(): return lambda v: lax.ppermute(v, 'tm', route)]
  transfers between devices with their start and end apart: 9 -> 9, of which waited for: 4 -> 5; matrix products, arithmetic and copies ran while one was open for 0% -> 0% of each run, Pallas kernels for 22% -> 24%
where the time goes in v1:
time: 58.8 us; the launch traced here: 57.8 us
  Pallas kernels  32.8 us (56%)
  starting transfers between devices  12.4 us (21%)
  waiting for transfers between devices  8.94 us (15%)
  between operations  1.4 us (2%)
  local copies, waits for them, and re-layouts  1.3 us (2%)
  other arithmetic  0.93 us (2%)
    pallas_call x2, Pallas kernels, by_tap(): pl.pallas_call(by_tap_kernel, grid=(count,), in_specs=[pl.BlockSpec((1, g...  13.7 us
    pallas_call x1, Pallas kernels, pos_conv(): pl.pallas_call(functools.partial(pos_conv_kernel, n_rec, early, phases, s...  11.2 us
    ppermute x3, starting transfers between devices, on_device(): lax.ppermute(p, 'grp', [(i ^ d, i) for i in range(grp)])  5.83 us
    pallas_call x1, Pallas kernels, front(): pl.pallas_call(front_kernel, grid=(1,), in_specs=[far, pl.BlockSpec(nxt.s...  5.44 us
    ppermute x1, waiting for transfers between devices, on_device(): edge = lax.ppermute(features[:, :1, :], 'tm', back)  3.81 us
    ppermute x2, starting transfers between devices, from_block(): return lambda v: lax.ppermute(v, 'tm', route)  3.38 us
    ppermute x3, waiting for transfers between devices, on_device(): totals = totals + lax.ppermute(own, 'grp', [(i ^ d, i) for i in range(grp)])  3 us
    pallas_call x1, Pallas kernels, project(): pl.pallas_call(functools.partial(project_kernel, n_dest, groups, tuples,...  2.47 us
  transfers between devices with their start and end apart: 9, of which 5 were waited for; matrix products, arithmetic and copies ran while one was open for 0% of the time, Pallas kernels for 24%

profile of v1, /device:TPU:0, one launch (start us, length us, event | category | flops | bytes accessed | tf_op | source)
XLA Modules:
  0.0 57.8 jit_solution(8401583065047776021)
XLA Ops:
  0.0 0.7 %slice.9 = bf16[1,1,512]{2,1,0:T(2,128)(2,1)S(1)} slice(bf16[1,1024,512]{2,1,0:T(8,128)(2,1)} %feat.1), slice={[0:1], [0:1], [0:512]} | slice | bytes 2048 | tf_op jit(solution)/shard_map/slice | solution.py:359
  0.7 1.3 %collective-permute-start.21 = (bf16[1,1,512]{2,1,0:T(2,128)(2,1)S(1)}, bf16[1,1,512]{2,1,0:T(2,128)(2,1)S(1)}, u32[]{:S(2)}, u32[]{:S(2)}) collective-permute-start(bf16[1,1,512]{2,1,0:T(2,128)(2,1)S(1)} %slice.9), channel_id=1, source_target_pairs={{4,0},{8,4},{12,8},{16,12},{20,16},{24,20},{28,24},{5,1},{9,5},{13... | collective-permute-start | bytes 3080 | tf_op jit(solution)/shard_map/ppermute | solution.py:359
  3.3 3.8 %collective-permute-done.21.nxt = bf16[1,1,512]{2,1,0:T(2,128)(2,1)S(1)} collective-permute-done((bf16[1,1,512]{2,1,0:T(2,128)(2,1)S(1)}, bf16[1,1,512]{2,1,0:T(2,128)(2,1)S(1)}, u32[]{:S(2)}, u32[]{:S(2)}) %collective-permute-start.21) | collective-permute-done | bytes 1056 | tf_op jit(solution)/shard_map/ppermute | solution.py:359
  7.1 0.0 copy-start.5
  7.1 0.6 copy-done.5
  7.7 5.4 %front.1 = (bf16[128,512]{1,0:T(8,128)(2,1)S(1)}, bf16[64,512]{1,0:T(8,128)(2,1)S(1)}, bf16[64,512]{1,0:T(8,128)(2,1)S(1)}) custom-call(bf16[1,1024,512]{2,1,0:T(8,128)(2,1)} %feat.1, bf16[1,1,512]{2,1,0:T(2,128)(2,1)} %copy-done.5, bf16[1536,512]{1,0:T(8,128)(2,1)} %w5.1, bf16[1024,512]{1,0:T(8,128)(2,1)} %w6.1, bf16[1024,512]{1,0:T(8,128)(2,1)} %w7.1, ...), custom_call_target="tpu_custom_call" | custom-call | flops 4831838208 | bytes 8388608 | tf_op jit(solution)/shard_map/front/pallas_call | solution.py:89
  13.1 0.0 copy-start
  13.2 0.0 copy-start.1
  13.2 10.5 %conditional.1 = (bf16[128,512]{1,0:T(8,128)(2,1)S(1)}, bf16[128,512]{1,0:T(8,128)(2,1)}, bf16[64,512]{1,0:T(8,128)(2,1)}, bf16[2,10240,128]{2,1,0:T(8,128)(2,1)}) conditional(s32[]{:T(128)} %clamp.3, (bf16[128,512]{1,0:T(8,128)(2,1)S(1)}, bf16[64,512]{1,0:T(8,128)(2,1)S(1)}, ...), branch_computations={%region_0.1_spmd, %region_1.2_spmd, %region_2.3_spmd, %region_3.4_... | conditional | bytes 22544536 | solution.py:390
  13.2 3.4 %collective-permute-start = (bf16[128,512]{1,0:T(8,128)(2,1)S(1)}, bf16[128,512]{1,0:T(8,128)(2,1)}, u32[]{:S(2)}, u32[]{:S(2)}) collective-permute-start(bf16[128,512]{1,0:T(8,128)(2,1)S(1)} %get-tuple-element.105), channel_id=1, source_target_pairs={{4,0},{8,4},{12,8},{16,12},{20,16},{24,20},{28,24},{0,28},{5,1},{9... | collective-permute-start | bytes 393224 | tf_op jit(solution)/shard_map/cond/branch_0_fun/ppermute | solution.py:375
  16.6 0.0 collective-permute-start.1
  16.6 6.8 %by_tap_0.8 = bf16[2,10240,128]{2,1,0:T(8,128)(2,1)} custom-call(bf16[4,80,80,128]{3,2,1,0:T(8,128)(2,1)} %get-tuple-element.55.w), custom_call_target="tpu_custom_call" | custom-call | bytes 20971520 | tf_op jit(solution)/shard_map/cond/branch_0_fun/by_tap_0/pallas_call | solution.py:194
  23.4 0.3 collective-permute-done.1
  23.7 0.0 collective-permute-done
  23.7 0.0 copy-done
  23.7 0.0 copy-done.1
  23.7 2.5 %project_window.1 = (bf16[4,88,256]{2,1,0:T(8,128)(2,1)S(1)}, bf16[4,88,256]{2,1,0:T(8,128)(2,1)S(1)}, bf16[4,88,256]{2,1,0:T(8,128)(2,1)S(1)}, bf16[4,88,256]{2,1,0:T(8,128)(2,1)S(1)}) custom-call(s32[1]{0:T(128)S(6)} %copy.50.crops, s32[1]{0:T(128)S(6)} %copy.49.lengths, bf16[128,512]{1,0:T(8,128)(2,1)S(1)} %get-tuple-element.93.b0, ...), custom_call_target="tpu_custom_call" | custom-call | tf_op jit(solution)/shard_map/project_window/pallas_call | solution.py:163
  26.2 1.8 %collective-permute-start.22 = (bf16[4,88,256]{2,1,0:T(8,128)(2,1)S(1)}, bf16[4,88,256]{2,1,0:T(8,128)(2,1)S(1)}, u32[]{:S(2)}, u32[]{:S(2)}) collective-permute-start(bf16[4,88,256]{2,1,0:T(8,128)(2,1)S(1)} %get-tuple-element.97), channel_id=1, source_target_pairs={{1,0},{0,1},{3,2},{2,3},{5,4},{4,5},{7,6},{6,7},{9,8},{8,9},{11,10... | collective-permute-start | bytes 540680 | tf_op jit(solution)/shard_map/ppermute | solution.py:407
  28.0 3.9 %collective-permute-start.23 = (bf16[4,88,256]{2,1,0:T(8,128)(2,1)S(1)}, bf16[4,88,256]{2,1,0:T(8,128)(2,1)S(1)}, u32[]{:S(2)}, u32[]{:S(2)}) collective-permute-start(bf16[4,88,256]{2,1,0:T(8,128)(2,1)S(1)} %get-tuple-element.98), channel_id=1, source_target_pairs={{2,0},{3,1},{0,2},{1,3},{6,4},{7,5},{4,6},{5,7},{10,8},{11,9},{8,1... | collective-permute-start | bytes 540680 | tf_op jit(solution)/shard_map/ppermute | solution.py:407
  31.9 0.0 copy-start.2
  31.9 0.1 collective-permute-start.24
  32.0 6.8 %by_tap_2.1.refs_5_ = bf16[2,10240,128]{2,1,0:T(8,128)(2,1)} custom-call(bf16[4,80,80,128]{3,2,1,0:T(8,128)(2,1)} %bitcast.12), custom_call_target="tpu_custom_call" | custom-call | bytes 20971520 | tf_op jit(solution)/shard_map/by_tap_2/pallas_call | solution.py:194
  38.9 0.0 collective-permute-done.22.refs_1_
  38.9 0.0 collective-permute-done.23.refs_2_
  38.9 1.8 %collective-permute-done.24.refs_3_ = bf16[4,88,256]{2,1,0:T(8,128)(2,1)S(1)} collective-permute-done((bf16[4,88,256]{2,1,0:T(8,128)(2,1)S(1)}, bf16[4,88,256]{2,1,0:T(8,128)(2,1)S(1)}, u32[]{:S(2)}, u32[]{:S(2)}) %collective-permute-start.24) | collective-permute-done | bytes 180256 | tf_op jit(solution)/shard_map/ppermute | solution.py:407
  40.7 0.0 copy-done.2
  40.7 0.0 copy-start.3
  40.7 0.0 copy-start.4
  40.7 11.2 %pos_conv.1 = (f32[4,320,128]{2,1,0:T(8,128)S(1)}, f32[8,128]{1,0:T(8,128)S(1)}) custom-call(bf16[4,88,256]{2,1,0:T(8,128)(2,1)S(1)} %get-tuple-element.96.refs_0_, bf16[4,88,256]{2,1,0:T(8,128)(2,1)S(1)} %collective-permute-done.22.refs_1_, bf16[4,88,256]{2,1,0:T(8,128)(2,1)S(1)} %collective-permute-done.23.refs_2_, ...), custom_call_target="tpu_custom_call" | custom-call | tf_op jit(solution)/shard_map/pos_conv/pallas_call | solution.py:304
  51.9 0.2 collective-permute-start.25
  52.1 1.7 %collective-permute-start.26 = (f32[8,128]{1,0:T(8,128)S(1)}, f32[8,128]{1,0:T(8,128)S(1)}, u32[]{:S(2)}, u32[]{:S(2)}) collective-permute-start(f32[8,128]{1,0:T(8,128)S(1)} %get-tuple-element.102), channel_id=1, source_target_pairs={{2,0},{3,1},{0,2},{1,3},{6,4},{7,5},{4,6},{5,7},{10,8},{11,9},{8,1... | collective-permute-start | bytes 12296 | tf_op jit(solution)/shard_map/ppermute | solution.py:415
  53.9 0.0 collective-permute-start.27
  53.9 0.0 collective-permute-done.25
  53.9 1.9 %collective-permute-done.26 = f32[8,128]{1,0:T(8,128)S(1)} collective-permute-done((f32[8,128]{1,0:T(8,128)S(1)}, f32[8,128]{1,0:T(8,128)S(1)}, u32[]{:S(2)}, u32[]{:S(2)}) %collective-permute-start.26) | collective-permute-done | bytes 4128 | tf_op jit(solution)/shard_map/ppermute | solution.py:415
  55.8 1.1 %collective-permute-done.27 = f32[8,128]{1,0:T(8,128)S(1)} collective-permute-done((f32[8,128]{1,0:T(8,128)S(1)}, f32[8,128]{1,0:T(8,128)S(1)}, u32[]{:S(2)}, u32[]{:S(2)}) %collective-permute-start.27) | collective-permute-done | bytes 4128 | tf_op jit(solution)/shard_map/ppermute | solution.py:415
  56.9 0.0 copy-done.3
  56.9 0.0 copy-done.4
  56.9 0.9 %fusion = bf16[4,128,320]{1,2,0:T(8,128)(2,1)} fusion(f32[4,320,128]{2,1,0:T(8,128)S(1)} %get-tuple-element.101, f32[320]{0:T(512)S(1)} %copy-done.3, f32[320]{0:T(512)S(1)} %copy-done.4, f32[4,128]{1,0:T(4,128)S(1)} %get-tuple-element.104, f32[4,128]{1,0:T(4,128)S(1)} %get-tuple-element.103), kind=kLoop, calls=%fused_computation.1 | loop fusion | flops 819200 | bytes 989696 | tf_op jit(solution)/shard_map/transpose | solution.py:421
  (2 shorter events, 0.0 us)
Async XLA Ops:
  0.7 6.4 %collective-permute-start.21 = (bf16[1,1,512]{2,1,0:T(2,128)(2,1)S(1)}, bf16[1,1,512]{2,1,0:T(2,128)(2,1)S(1)}, u32[]{:S(2)}, u32[]{:S(2)}) collective-permute-start(bf16[1,1,512]{2,1,0:T(2,128)(2,1)S(1)} %slice.9), channel_id=1, source_target_pairs={{4,0},{8,4},{12,8},{16,12},{20,16},{24,20},{28,24},{5,1},{9,5},{13... | collective-permute-start | bytes 3080 | tf_op jit(solution)/shard_map/ppermute | solution.py:359
  7.1 0.6 copy-start.5
  13.1 10.6 %copy-start = (bf16[512,1280]{1,0:T(8,128)(2,1)S(1)}, bf16[512,1280]{1,0:T(8,128)(2,1)}, u32[]{:S(2)}) copy-start(bf16[512,1280]{1,0:T(8,128)(2,1)} %w.1) | copy-start | bytes 3932164
  13.2 10.5 %copy-start.1 = (f32[1280]{0:T(1024)S(1)}, f32[1280]{0:T(1024)}, u32[]{:S(2)}) copy-start(f32[1280]{0:T(1024)} %bias.1) | copy-start | bytes 15364
  13.2 10.5 %collective-permute-start = (bf16[128,512]{1,0:T(8,128)(2,1)S(1)}, bf16[128,512]{1,0:T(8,128)(2,1)}, u32[]{:S(2)}, u32[]{:S(2)}) collective-permute-start(bf16[128,512]{1,0:T(8,128)(2,1)S(1)} %get-tuple-element.105), channel_id=1, source_target_pairs={{4,0},{8,4},{12,8},{16,12},{20,16},{24,20},{28,24},{0,28},{5,1},{9... | collective-permute-start | bytes 393224 | tf_op jit(solution)/shard_map/cond/branch_0_fun/ppermute | solution.py:375
  16.6 7.1 %collective-permute-start.1 = (bf16[64,512]{1,0:T(8,128)(2,1)S(1)}, bf16[64,512]{1,0:T(8,128)(2,1)}, u32[]{:S(2)}, u32[]{:S(2)}) collective-permute-start(bf16[64,512]{1,0:T(8,128)(2,1)S(1)} %get-tuple-element.54), channel_id=1, source_target_pairs={{28,0},{0,4},{4,8},{8,12},{12,16},{16,20},{20,24},{24,28},{29,1},{... | collective-permute-start | bytes 196616 | tf_op jit(solution)/shard_map/cond/branch_0_fun/ppermute | solution.py:375
  26.2 12.7 %collective-permute-start.22 = (bf16[4,88,256]{2,1,0:T(8,128)(2,1)S(1)}, bf16[4,88,256]{2,1,0:T(8,128)(2,1)S(1)}, u32[]{:S(2)}, u32[]{:S(2)}) collective-permute-start(bf16[4,88,256]{2,1,0:T(8,128)(2,1)S(1)} %get-tuple-element.97), channel_id=1, source_target_pairs={{1,0},{0,1},{3,2},{2,3},{5,4},{4,5},{7,6},{6,7},{9,8},{8,9},{11,10... | collective-permute-start | bytes 540680 | tf_op jit(solution)/shard_map/ppermute | solution.py:407
  28.0 10.8 %collective-permute-start.23 = (bf16[4,88,256]{2,1,0:T(8,128)(2,1)S(1)}, bf16[4,88,256]{2,1,0:T(8,128)(2,1)S(1)}, u32[]{:S(2)}, u32[]{:S(2)}) collective-permute-start(bf16[4,88,256]{2,1,0:T(8,128)(2,1)S(1)} %get-tuple-element.98), channel_id=1, source_target_pairs={{2,0},{3,1},{0,2},{1,3},{6,4},{7,5},{4,6},{5,7},{10,8},{11,9},{8,1... | collective-permute-start | bytes 540680 | tf_op jit(solution)/shard_map/ppermute | solution.py:407
  31.9 8.7 %copy-start.2 = (f32[320]{0:T(512)S(1)}, f32[320]{0:T(512)}, u32[]{:S(2)}) copy-start(f32[320]{0:T(512)} %refs_6_.1) | copy-start | bytes 3844
  31.9 8.7 %collective-permute-start.24 = (bf16[4,88,256]{2,1,0:T(8,128)(2,1)S(1)}, bf16[4,88,256]{2,1,0:T(8,128)(2,1)S(1)}, u32[]{:S(2)}, u32[]{:S(2)}) collective-permute-start(bf16[4,88,256]{2,1,0:T(8,128)(2,1)S(1)} %get-tuple-element.99), channel_id=1, source_target_pairs={{3,0},{2,1},{1,2},{0,3},{7,4},{6,5},{5,6},{4,7},{11,8},{10,9},{9,1... | collective-permute-start | bytes 540680 | tf_op jit(solution)/shard_map/ppermute | solution.py:407
  40.7 16.2 %copy-start.3 = (f32[320]{0:T(512)S(1)}, f32[320]{0:T(512)}, u32[]{:S(2)}) copy-start(f32[320]{0:T(512)} %param.37) | copy-start | bytes 3844
  40.7 16.2 %copy-start.4 = (f32[320]{0:T(512)S(1)}, f32[320]{0:T(512)}, u32[]{:S(2)}) copy-start(f32[320]{0:T(512)} %param.36) | copy-start | bytes 3844
  51.9 2.0 %collective-permute-start.25 = (f32[8,128]{1,0:T(8,128)S(1)}, f32[8,128]{1,0:T(8,128)S(1)}, u32[]{:S(2)}, u32[]{:S(2)}) collective-permute-start(f32[8,128]{1,0:T(8,128)S(1)} %get-tuple-element.102), channel_id=1, source_target_pairs={{1,0},{0,1},{3,2},{2,3},{5,4},{4,5},{7,6},{6,7},{9,8},{8,9},{11,10... | collective-permute-start | bytes 12296 | tf_op jit(solution)/shard_map/ppermute | solution.py:415
  52.1 3.6 %collective-permute-start.26 = (f32[8,128]{1,0:T(8,128)S(1)}, f32[8,128]{1,0:T(8,128)S(1)}, u32[]{:S(2)}, u32[]{:S(2)}) collective-permute-start(f32[8,128]{1,0:T(8,128)S(1)} %get-tuple-element.102), channel_id=1, source_target_pairs={{2,0},{3,1},{0,2},{1,3},{6,4},{7,5},{4,6},{5,7},{10,8},{11,9},{8,1... | collective-permute-start | bytes 12296 | tf_op jit(solution)/shard_map/ppermute | solution.py:415
  53.9 3.0 %collective-permute-start.27 = (f32[8,128]{1,0:T(8,128)S(1)}, f32[8,128]{1,0:T(8,128)S(1)}, u32[]{:S(2)}, u32[]{:S(2)}) collective-permute-start(f32[8,128]{1,0:T(8,128)S(1)} %get-tuple-element.102), channel_id=1, source_target_pairs={{3,0},{2,1},{1,2},{0,3},{7,4},{6,5},{5,6},{4,7},{11,8},{10,9},{9,1... | collective-permute-start | bytes 12296 | tf_op jit(solution)/shard_map/ppermute | solution.py:415

commit v2 on v1

--- a/solution.py
+++ b/solution.py
@@ -378,7 +378,7 @@
         block, odd = first // 2, first % 2
 
         def run(v, low, high, w):
-            pair = [from_block(block + odd + i)(v) for i in range(2)]
+            pair = [from_block(block + odd + i)(v) for i in (1, 0)]
             extra = from_block(block)(high) if odd else from_block(block + 2)(low)
             return *pair, extra, by_tap(w, 0, early)
 
@@ -395,6 +395,7 @@
         high,
         by_channel,
     )
+    blocks = (blocks[1], blocks[0], blocks[2])
 
     n_rec = grp
     phases = 16 // n_rec

time: 58.8 us -> 56.3 us (0.957); the launches traced: 57.8 us -> 56.5 us
  starting transfers between devices: 12.4 us -> 11.1 us
    ppermute x3, starting transfers between devices: 5.83 us -> 4.47 us  [on_device(): lax.ppermute(p, 'grp', [(i ^ d, i) for i in range(grp)])]
where the time goes in v2:
time: 56.3 us; the launch traced here: 56.5 us
  Pallas kernels  32.8 us (58%)
  starting transfers between devices  11.1 us (20%)
  waiting for transfers between devices  8.94 us (16%)
  between operations  1.4 us (2%)
  local copies, waits for them, and re-layouts  1.3 us (2%)
  other arithmetic  0.93 us (2%)
    pallas_call x2, Pallas kernels, by_tap(): pl.pallas_call(by_tap_kernel, grid=(count,), in_specs=[pl.BlockSpec((1, g...  13.7 us
    pallas_call x1, Pallas kernels, pos_conv(): pl.pallas_call(functools.partial(pos_conv_kernel, n_rec, early, phases, s...  11.2 us
    pallas_call x1, Pallas kernels, front(): pl.pallas_call(front_kernel, grid=(1,), in_specs=[far, pl.BlockSpec(nxt.s...  5.44 us
    ppermute x3, starting transfers between devices, on_device(): lax.ppermute(p, 'grp', [(i ^ d, i) for i in range(grp)])  4.47 us
    ppermute x1, waiting for transfers between devices, on_device(): edge = lax.ppermute(features[:, :1, :], 'tm', back)  3.81 us
    ppermute x2, starting transfers between devices, from_block(): return lambda v: lax.ppermute(v, 'tm', route)  3.38 us
    ppermute x3, waiting for transfers between devices, on_device(): totals = totals + lax.ppermute(own, 'grp', [(i ^ d, i) for i in range(grp)])  2.98 us
    pallas_call x1, Pallas kernels, project(): pl.pallas_call(functools.partial(project_kernel, n_dest, groups, tuples,...  2.47 us
  transfers between devices with their start and end apart: 9, of which 5 were waited for; matrix products, arithmetic and copies ran while one was open for 0% of the time, Pallas kernels for 24%

profile of v2, /device:TPU:0, one launch (start us, length us, event | category | flops | bytes accessed | tf_op | source)
XLA Modules:
  0.0 56.5 jit_solution(938596473473063254)
XLA Ops:
  0.0 0.7 %slice.9 = bf16[1,1,512]{2,1,0:T(2,128)(2,1)S(1)} slice(bf16[1,1024,512]{2,1,0:T(8,128)(2,1)} %feat.1), slice={[0:1], [0:1], [0:512]} | slice | bytes 2048 | tf_op jit(solution)/shard_map/slice | solution.py:359
  0.7 1.3 %collective-permute-start.21 = (bf16[1,1,512]{2,1,0:T(2,128)(2,1)S(1)}, bf16[1,1,512]{2,1,0:T(2,128)(2,1)S(1)}, u32[]{:S(2)}, u32[]{:S(2)}) collective-permute-start(bf16[1,1,512]{2,1,0:T(2,128)(2,1)S(1)} %slice.9), channel_id=1, source_target_pairs={{4,0},{8,4},{12,8},{16,12},{20,16},{24,20},{28,24},{5,1},{9,5},{13... | collective-permute-start | bytes 3080 | tf_op jit(solution)/shard_map/ppermute | solution.py:359
  3.3 3.8 %collective-permute-done.21.nxt = bf16[1,1,512]{2,1,0:T(2,128)(2,1)S(1)} collective-permute-done((bf16[1,1,512]{2,1,0:T(2,128)(2,1)S(1)}, bf16[1,1,512]{2,1,0:T(2,128)(2,1)S(1)}, u32[]{:S(2)}, u32[]{:S(2)}) %collective-permute-start.21) | collective-permute-done | bytes 1056 | tf_op jit(solution)/shard_map/ppermute | solution.py:359
  7.1 0.0 copy-start.5
  7.1 0.6 %copy-done.5 = bf16[1,1,512]{2,1,0:T(2,128)(2,1)} copy-done((bf16[1,1,512]{2,1,0:T(2,128)(2,1)}, bf16[1,1,512]{2,1,0:T(2,128)(2,1)S(1)}, u32[]{:S(2)}) %copy-start.5) | copy-done | bytes 1048
  7.7 5.4 %front.1 = (bf16[128,512]{1,0:T(8,128)(2,1)S(1)}, bf16[64,512]{1,0:T(8,128)(2,1)S(1)}, bf16[64,512]{1,0:T(8,128)(2,1)S(1)}) custom-call(bf16[1,1024,512]{2,1,0:T(8,128)(2,1)} %feat.1, bf16[1,1,512]{2,1,0:T(2,128)(2,1)} %copy-done.5, bf16[1536,512]{1,0:T(8,128)(2,1)} %w5.1, bf16[1024,512]{1,0:T(8,128)(2,1)} %w6.1, bf16[1024,512]{1,0:T(8,128)(2,1)} %w7.1, ...), custom_call_target="tpu_custom_call" | custom-call | flops 4831838208 | bytes 8388608 | tf_op jit(solution)/shard_map/front/pallas_call | solution.py:89
  13.1 0.0 copy-start
  13.2 0.0 copy-start.1
  13.2 10.5 %conditional.1 = (bf16[128,512]{1,0:T(8,128)(2,1)}, bf16[128,512]{1,0:T(8,128)(2,1)S(1)}, bf16[64,512]{1,0:T(8,128)(2,1)}, bf16[2,10240,128]{2,1,0:T(8,128)(2,1)}) conditional(s32[]{:T(128)} %clamp.3, (bf16[128,512]{1,0:T(8,128)(2,1)S(1)}, bf16[64,512]{1,0:T(8,128)(2,1)S(1)}, ...), branch_computations={%region_0.1_spmd, %region_1.2_spmd, %region_2.3_spmd, %region_3.4_... | conditional | bytes 22544536 | solution.py:390
  13.2 3.4 %collective-permute-start = (bf16[128,512]{1,0:T(8,128)(2,1)S(1)}, bf16[128,512]{1,0:T(8,128)(2,1)}, u32[]{:S(2)}, u32[]{:S(2)}) collective-permute-start(bf16[128,512]{1,0:T(8,128)(2,1)S(1)} %get-tuple-element.106), channel_id=1, source_target_pairs={{4,0},{8,4},{12,8},{16,12},{20,16},{24,20},{28,24},{0,28},{5,1},{9... | collective-permute-start | bytes 393224 | tf_op jit(solution)/shard_map/cond/branch_0_fun/ppermute | solution.py:375
  16.6 0.0 collective-permute-start.1
  16.6 6.8 %by_tap_0.8 = bf16[2,10240,128]{2,1,0:T(8,128)(2,1)} custom-call(bf16[4,80,80,128]{3,2,1,0:T(8,128)(2,1)} %get-tuple-element.55.w), custom_call_target="tpu_custom_call" | custom-call | bytes 20971520 | tf_op jit(solution)/shard_map/cond/branch_0_fun/by_tap_0/pallas_call | solution.py:194
  23.4 0.3 collective-permute-done.1
  23.7 0.0 collective-permute-done
  23.7 0.0 copy-done
  23.7 0.0 copy-done.1
  23.7 2.5 %project_window.1 = (bf16[4,88,256]{2,1,0:T(8,128)(2,1)S(1)}, bf16[4,88,256]{2,1,0:T(8,128)(2,1)S(1)}, bf16[4,88,256]{2,1,0:T(8,128)(2,1)S(1)}, bf16[4,88,256]{2,1,0:T(8,128)(2,1)S(1)}) custom-call(s32[1]{0:T(128)S(6)} %copy.50.crops, s32[1]{0:T(128)S(6)} %copy.49.lengths, bf16[128,512]{1,0:T(8,128)(2,1)S(1)} %get-tuple-element.93.b0, ...), custom_call_target="tpu_custom_call" | custom-call | tf_op jit(solution)/shard_map/project_window/pallas_call | solution.py:163
  26.2 0.4 collective-permute-start.22
  26.6 4.0 %collective-permute-start.23 = (bf16[4,88,256]{2,1,0:T(8,128)(2,1)S(1)}, bf16[4,88,256]{2,1,0:T(8,128)(2,1)S(1)}, u32[]{:S(2)}, u32[]{:S(2)}) collective-permute-start(bf16[4,88,256]{2,1,0:T(8,128)(2,1)S(1)} %get-tuple-element.98), channel_id=1, source_target_pairs={{2,0},{3,1},{0,2},{1,3},{6,4},{7,5},{4,6},{5,7},{10,8},{11,9},{8,1... | collective-permute-start | bytes 540680 | tf_op jit(solution)/shard_map/ppermute | solution.py:408
  30.6 0.0 copy-start.2
  30.6 0.1 collective-permute-start.24
  30.7 6.8 %by_tap_2.1.refs_5_ = bf16[2,10240,128]{2,1,0:T(8,128)(2,1)} custom-call(bf16[4,80,80,128]{3,2,1,0:T(8,128)(2,1)} %bitcast.12), custom_call_target="tpu_custom_call" | custom-call | bytes 20971520 | tf_op jit(solution)/shard_map/by_tap_2/pallas_call | solution.py:194
  37.5 0.0 collective-permute-done.22.refs_1_
  37.5 0.0 collective-permute-done.23.refs_2_
  37.5 1.8 %collective-permute-done.24.refs_3_ = bf16[4,88,256]{2,1,0:T(8,128)(2,1)S(1)} collective-permute-done((bf16[4,88,256]{2,1,0:T(8,128)(2,1)S(1)}, bf16[4,88,256]{2,1,0:T(8,128)(2,1)S(1)}, u32[]{:S(2)}, u32[]{:S(2)}) %collective-permute-start.24) | collective-permute-done | bytes 180256 | tf_op jit(solution)/shard_map/ppermute | solution.py:408
  39.3 0.0 copy-done.2
  39.3 0.0 copy-start.3
  39.3 0.0 copy-start.4
  39.4 11.2 %pos_conv.1 = (f32[4,320,128]{2,1,0:T(8,128)S(1)}, f32[8,128]{1,0:T(8,128)S(1)}) custom-call(bf16[4,88,256]{2,1,0:T(8,128)(2,1)S(1)} %get-tuple-element.96.refs_0_, bf16[4,88,256]{2,1,0:T(8,128)(2,1)S(1)} %collective-permute-done.22.refs_1_, bf16[4,88,256]{2,1,0:T(8,128)(2,1)S(1)} %collective-permute-done.23.refs_2_, ...), custom_call_target="tpu_custom_call" | custom-call | tf_op jit(solution)/shard_map/pos_conv/pallas_call | solution.py:304
  50.6 0.2 collective-permute-start.25
  50.8 1.7 %collective-permute-start.26 = (f32[8,128]{1,0:T(8,128)S(1)}, f32[8,128]{1,0:T(8,128)S(1)}, u32[]{:S(2)}, u32[]{:S(2)}) collective-permute-start(f32[8,128]{1,0:T(8,128)S(1)} %get-tuple-element.102), channel_id=1, source_target_pairs={{2,0},{3,1},{0,2},{1,3},{6,4},{7,5},{4,6},{5,7},{10,8},{11,9},{8,1... | collective-permute-start | bytes 12296 | tf_op jit(solution)/shard_map/ppermute | solution.py:416
  52.5 0.0 collective-permute-start.27
  52.6 0.0 collective-permute-done.25
  52.6 1.8 %collective-permute-done.26 = f32[8,128]{1,0:T(8,128)S(1)} collective-permute-done((f32[8,128]{1,0:T(8,128)S(1)}, f32[8,128]{1,0:T(8,128)S(1)}, u32[]{:S(2)}, u32[]{:S(2)}) %collective-permute-start.26) | collective-permute-done | bytes 4128 | tf_op jit(solution)/shard_map/ppermute | solution.py:416
  54.4 1.2 %collective-permute-done.27 = f32[8,128]{1,0:T(8,128)S(1)} collective-permute-done((f32[8,128]{1,0:T(8,128)S(1)}, f32[8,128]{1,0:T(8,128)S(1)}, u32[]{:S(2)}, u32[]{:S(2)}) %collective-permute-start.27) | collective-permute-done | bytes 4128 | tf_op jit(solution)/shard_map/ppermute | solution.py:416
  55.6 0.0 copy-done.3
  55.6 0.0 copy-done.4
  55.6 0.9 %fusion = bf16[4,128,320]{1,2,0:T(8,128)(2,1)} fusion(f32[4,320,128]{2,1,0:T(8,128)S(1)} %get-tuple-element.101, f32[320]{0:T(512)S(1)} %copy-done.3, f32[320]{0:T(512)S(1)} %copy-done.4, f32[4,128]{1,0:T(4,128)S(1)} %get-tuple-element.104, f32[4,128]{1,0:T(4,128)S(1)} %get-tuple-element.103), kind=kLoop, calls=%fused_computation.1 | loop fusion | flops 819200 | bytes 989696 | tf_op jit(solution)/shard_map/transpose | solution.py:422
  (2 shorter events, 0.0 us)
Async XLA Ops:
  0.7 6.4 %collective-permute-start.21 = (bf16[1,1,512]{2,1,0:T(2,128)(2,1)S(1)}, bf16[1,1,512]{2,1,0:T(2,128)(2,1)S(1)}, u32[]{:S(2)}, u32[]{:S(2)}) collective-permute-start(bf16[1,1,512]{2,1,0:T(2,128)(2,1)S(1)} %slice.9), channel_id=1, source_target_pairs={{4,0},{8,4},{12,8},{16,12},{20,16},{24,20},{28,24},{5,1},{9,5},{13... | collective-permute-start | bytes 3080 | tf_op jit(solution)/shard_map/ppermute | solution.py:359
  7.1 0.6 %copy-start.5 = (bf16[1,1,512]{2,1,0:T(2,128)(2,1)}, bf16[1,1,512]{2,1,0:T(2,128)(2,1)S(1)}, u32[]{:S(2)}) copy-start(bf16[1,1,512]{2,1,0:T(2,128)(2,1)S(1)} %collective-permute-done.21.nxt) | copy-start | bytes 3076
  13.1 10.6 %copy-start = (bf16[512,1280]{1,0:T(8,128)(2,1)S(1)}, bf16[512,1280]{1,0:T(8,128)(2,1)}, u32[]{:S(2)}) copy-start(bf16[512,1280]{1,0:T(8,128)(2,1)} %w.1) | copy-start | bytes 3932164
  13.2 10.6 %copy-start.1 = (f32[1280]{0:T(1024)S(1)}, f32[1280]{0:T(1024)}, u32[]{:S(2)}) copy-start(f32[1280]{0:T(1024)} %bias.1) | copy-start | bytes 15364
  13.2 10.5 %collective-permute-start = (bf16[128,512]{1,0:T(8,128)(2,1)S(1)}, bf16[128,512]{1,0:T(8,128)(2,1)}, u32[]{:S(2)}, u32[]{:S(2)}) collective-permute-start(bf16[128,512]{1,0:T(8,128)(2,1)S(1)} %get-tuple-element.106), channel_id=1, source_target_pairs={{4,0},{8,4},{12,8},{16,12},{20,16},{24,20},{28,24},{0,28},{5,1},{9... | collective-permute-start | bytes 393224 | tf_op jit(solution)/shard_map/cond/branch_0_fun/ppermute | solution.py:375
  16.6 7.1 %collective-permute-start.1 = (bf16[64,512]{1,0:T(8,128)(2,1)S(1)}, bf16[64,512]{1,0:T(8,128)(2,1)}, u32[]{:S(2)}, u32[]{:S(2)}) collective-permute-start(bf16[64,512]{1,0:T(8,128)(2,1)S(1)} %get-tuple-element.54), channel_id=1, source_target_pairs={{28,0},{0,4},{4,8},{8,12},{12,16},{16,20},{20,24},{24,28},{29,1},{... | collective-permute-start | bytes 196616 | tf_op jit(solution)/shard_map/cond/branch_0_fun/ppermute | solution.py:375
  26.2 11.3 %collective-permute-start.22 = (bf16[4,88,256]{2,1,0:T(8,128)(2,1)S(1)}, bf16[4,88,256]{2,1,0:T(8,128)(2,1)S(1)}, u32[]{:S(2)}, u32[]{:S(2)}) collective-permute-start(bf16[4,88,256]{2,1,0:T(8,128)(2,1)S(1)} %get-tuple-element.97), channel_id=1, source_target_pairs={{1,0},{0,1},{3,2},{2,3},{5,4},{4,5},{7,6},{6,7},{9,8},{8,9},{11,10... | collective-permute-start | bytes 540680 | tf_op jit(solution)/shard_map/ppermute | solution.py:408
  26.6 10.9 %collective-permute-start.23 = (bf16[4,88,256]{2,1,0:T(8,128)(2,1)S(1)}, bf16[4,88,256]{2,1,0:T(8,128)(2,1)S(1)}, u32[]{:S(2)}, u32[]{:S(2)}) collective-permute-start(bf16[4,88,256]{2,1,0:T(8,128)(2,1)S(1)} %get-tuple-element.98), channel_id=1, source_target_pairs={{2,0},{3,1},{0,2},{1,3},{6,4},{7,5},{4,6},{5,7},{10,8},{11,9},{8,1... | collective-permute-start | bytes 540680 | tf_op jit(solution)/shard_map/ppermute | solution.py:408
  30.6 8.7 %copy-start.2 = (f32[320]{0:T(512)S(1)}, f32[320]{0:T(512)}, u32[]{:S(2)}) copy-start(f32[320]{0:T(512)} %refs_6_.1) | copy-start | bytes 3844
  30.6 8.7 %collective-permute-start.24 = (bf16[4,88,256]{2,1,0:T(8,128)(2,1)S(1)}, bf16[4,88,256]{2,1,0:T(8,128)(2,1)S(1)}, u32[]{:S(2)}, u32[]{:S(2)}) collective-permute-start(bf16[4,88,256]{2,1,0:T(8,128)(2,1)S(1)} %get-tuple-element.99), channel_id=1, source_target_pairs={{3,0},{2,1},{1,2},{0,3},{7,4},{6,5},{5,6},{4,7},{11,8},{10,9},{9,1... | collective-permute-start | bytes 540680 | tf_op jit(solution)/shard_map/ppermute | solution.py:408
  39.3 16.2 %copy-start.3 = (f32[320]{0:T(512)S(1)}, f32[320]{0:T(512)}, u32[]{:S(2)}) copy-start(f32[320]{0:T(512)} %param.37) | copy-start | bytes 3844
  39.3 16.2 %copy-start.4 = (f32[320]{0:T(512)S(1)}, f32[320]{0:T(512)}, u32[]{:S(2)}) copy-start(f32[320]{0:T(512)} %param.36) | copy-start | bytes 3844
  50.6 2.0 %collective-permute-start.25 = (f32[8,128]{1,0:T(8,128)S(1)}, f32[8,128]{1,0:T(8,128)S(1)}, u32[]{:S(2)}, u32[]{:S(2)}) collective-permute-start(f32[8,128]{1,0:T(8,128)S(1)} %get-tuple-element.102), channel_id=1, source_target_pairs={{1,0},{0,1},{3,2},{2,3},{5,4},{4,5},{7,6},{6,7},{9,8},{8,9},{11,10... | collective-permute-start | bytes 12296 | tf_op jit(solution)/shard_map/ppermute | solution.py:416
  50.8 3.6 %collective-permute-start.26 = (f32[8,128]{1,0:T(8,128)S(1)}, f32[8,128]{1,0:T(8,128)S(1)}, u32[]{:S(2)}, u32[]{:S(2)}) collective-permute-start(f32[8,128]{1,0:T(8,128)S(1)} %get-tuple-element.102), channel_id=1, source_target_pairs={{2,0},{3,1},{0,2},{1,3},{6,4},{7,5},{4,6},{5,7},{10,8},{11,9},{8,1... | collective-permute-start | bytes 12296 | tf_op jit(solution)/shard_map/ppermute | solution.py:416
  52.5 3.0 %collective-permute-start.27 = (f32[8,128]{1,0:T(8,128)S(1)}, f32[8,128]{1,0:T(8,128)S(1)}, u32[]{:S(2)}, u32[]{:S(2)}) collective-permute-start(f32[8,128]{1,0:T(8,128)S(1)} %get-tuple-element.102), channel_id=1, source_target_pairs={{3,0},{2,1},{1,2},{0,3},{7,4},{6,5},{5,6},{4,7},{11,8},{10,9},{9,1... | collective-permute-start | bytes 12296 | tf_op jit(solution)/shard_map/ppermute | solution.py:416
